TPU v7x, 128 devices: a whole 4x4x4 slice. The times are simulated.
128 devices in a mesh: dp: 8 (over z, core), expert: 16 (over y, x).
Axes of the slice: x: 4, y: 4, z: 4, core: 2. Of those that a mesh axis runs over, the one named last changes fastest.
Arguments:
- inputs: bfloat16 [16384, 2048], P(('dp', 'expert')), may hold values from -6 to 6
- out_grad: bfloat16 [16384, 2048], P(('dp', 'expert')), may hold values from -6 to 6
- combine: float32 [16384, 8], P(('dp', 'expert')), may hold values from 0 to 1, as said below
- routes: int32 [16384, 8], P(('dp', 'expert')), may hold values from 0 to 63, all different within a row; in each aligned block of 128 rows (0 to 127, 128 to 255, ...) at most 24 rows name the same one
- saved_hidden: bfloat16 [8, 64, 16, 24, 768], P('dp', 'expert'), may hold values from -6 to 6
- down_weight: bfloat16 [64, 2048, 768], P('expert'), may hold values from -0.21875 to 0.21875
- router_weight: bfloat16 [64, 2048], replicated, may hold values from -0.125 to 0.125
Outputs:
- hidden_grad: bfloat16 [8, 64, 16, 24, 768], P('dp', 'expert')
- down_grad: bfloat16 [64, 2048, 768], P('expert', 'dp')
- input_grad: bfloat16 [16384, 2048], P(('dp', 'expert'))
- router_grad: float32 [64, 2048], replicated
Inputs may be any that keep to these rules, and one draw needn't show every extreme that they name: `routes`: each token names 8 different experts; among the 128 tokens of one device no expert is named by more than 24 tokens, a bound that some block reaches. `combine`: each token's 8 weights are positive and sum to one.
All inputs are finite; a program needn't handle non-finite values.
Results may differ from a plain program's by a relative error of at most 0.017.
Values may be sent and summed in bfloat16 or wider, within the bound.
A program may use at most 128 MiB of HBM per device.

v0:
```python
import jax
import jax.numpy as jnp
from jax import lax
from jax.sharding import PartitionSpec as P


def make_marks(block_routes, total_experts):
    return block_routes[:, :, None] == jnp.arange(total_experts, dtype=jnp.int32)[None, None, :]


def slot_positions(route_marks):
    counts = jnp.sum(route_marks.astype(jnp.bfloat16), axis=1)
    token_order = jnp.arange(route_marks.shape[0], dtype=jnp.int32)
    earlier = (token_order[None, :] < token_order[:, None]).astype(jnp.bfloat16)
    before = jnp.dot(earlier, counts, preferred_element_type=jnp.float32)
    picked = jnp.sum(jnp.where(route_marks, before[:, None, :], 0.0), axis=2)
    return picked.astype(jnp.int32)


def pack_rows(scaled, lane_index, owner_slot, positions, local_experts, groups, capacity):
    width = scaled.shape[-1]
    flat_index = (owner_slot * groups + lane_index) * capacity + positions
    zero_rows = jnp.zeros((local_experts * groups * capacity, width), jnp.bfloat16)
    filled = zero_rows.at[flat_index.reshape(-1)].set(scaled.reshape(-1, width))
    return filled.reshape(local_experts, groups, capacity, width)


def local(inputs, out_grad, combine, routes, saved_hidden, down_weight, router_weight):
    token_count, width = out_grad.shape
    local_experts = down_weight.shape[0]
    total_experts = router_weight.shape[0]
    groups = lax.axis_size("expert")
    capacity = saved_hidden.shape[3]
    hidden_width = saved_hidden.shape[4]
    route_marks = make_marks(routes, total_experts)
    positions = slot_positions(route_marks)
    owner_dev = routes // local_experts
    owner_slot = routes % local_experts
    scaled = (combine[:, :, None] * out_grad[:, None, :].astype(jnp.float32)).astype(jnp.bfloat16)
    packed = pack_rows(scaled, owner_dev, owner_slot, positions, local_experts, groups, capacity)
    received = lax.all_to_all(packed, "expert", split_axis=1, concat_axis=1, tiled=True)
    hidden_local = saved_hidden[0]
    products_list = []
    hidden_list = []
    weight_terms = []
    for expert in range(local_experts):
        slot_rows = received[expert].reshape(groups * capacity, width)
        slot_acts = hidden_local[expert].reshape(groups * capacity, hidden_width)
        weight = down_weight[expert]
        recomputed = lax.dot_general(
            slot_acts, weight, (((1,), (1,)), ((), ())), preferred_element_type=jnp.float32
        )
        products_list.append(jnp.sum(recomputed * slot_rows.astype(jnp.float32), axis=1))
        hidden_list.append(
            jnp.dot(slot_rows, weight, preferred_element_type=jnp.float32).astype(jnp.bfloat16)
        )
        weight_terms.append(
            lax.dot_general(
                slot_rows, slot_acts, (((0,), (0,)), ((), ())), preferred_element_type=jnp.float32
            )
        )
    down_grad = lax.psum_scatter(
        jnp.stack(weight_terms).astype(jnp.bfloat16), "dp", scatter_dimension=1, tiled=True
    )
    hidden_grad = jnp.stack(hidden_list).reshape(1, local_experts, groups, capacity, hidden_width)
    slot_products = jnp.stack(products_list).reshape(local_experts, groups, capacity)
    returned = lax.all_to_all(slot_products, "expert", split_axis=1, concat_axis=1, tiled=True)
    pair_index = (owner_slot * groups + owner_dev) * capacity + positions
    pair_sums = returned.reshape(-1)[pair_index]
    logit_grad = pair_sums - combine * jnp.sum(pair_sums, axis=1, keepdims=True)
    dense_grad = jnp.sum(jnp.where(route_marks, logit_grad[:, :, None], 0.0), axis=1).astype(
        jnp.bfloat16
    )
    input_grad = jnp.dot(dense_grad, router_weight, preferred_element_type=jnp.float32).astype(
        jnp.bfloat16
    )
    router_part = lax.dot_general(
        dense_grad, inputs, (((0,), (0,)), ((), ())), preferred_element_type=jnp.float32
    )
    router_grad = lax.psum(router_part, ("dp", "expert"))
    return (hidden_grad, down_grad, input_grad, router_grad)


def solution(mesh):
    placed = (
        P(("dp", "expert"), None),
        P(("dp", "expert"), None),
        P(("dp", "expert"), None),
        P(("dp", "expert"), None),
        P("dp", "expert", None, None, None),
        P("expert", None, None),
        P(),
    )
    return jax.shard_map(
        local,
        mesh=mesh,
        in_specs=placed,
        out_specs=(
            P("dp", "expert", None, None, None),
            P("expert", "dp", None),
            P(("dp", "expert"), None),
            P(),
        ),
        check_vma=False,
    )
```

profile of v0, /device:TPU:1, one launch (start us, length us, event | category | flops | bytes accessed | tf_op | source)
XLA Modules:
  0.0 366.2 jit_solution(16921963926218966697)
XLA Ops:
  8.0 0.0 copy-start
  8.0 0.8 fusion.55
  8.8 0.1 fusion.56
  8.9 0.7 select_reduce_fusion.1
  9.7 0.7 compare_select_fusion.1
  10.4 0.1 copy.45
  10.5 0.1 reshape.82
  10.6 0.8 copy.46
  11.4 0.1 mul.48
  11.5 1.1 convert_element_type.50
  12.6 10.6 %scatter_custom_fusion = bf16[1536,2048]{1,0:T(8,128)(2,1)} fusion(s32[1024]{0:T(1024)S(1)} %bitcast.110, f32[128,2048]{1,0:T(8,128)S(1)} %convert_element_type.50, f32[1024]{0:T(1024)S(1)} %mul.48, bf16[]{:T(256)} %constant.31.clone.1), kind=kCustom, calls=%fused_computation.5 | custom fusion | flops 4194304 | bytes 7344130 | tf_op jit(solution)/shard_map/scatter | solution.py:24
  23.2 6.6 %copy.47 = bf16[4,16,24,2048]{3,2,0,1:T(8,128)(2,1)} copy(bf16[4,16,24,2048]{3,2,1,0:T(8,128)(2,1)} %bitcast.85) | data formatting | bytes 12582912 | tf_op jit(solution)/shard_map/reshape | solution.py:25
  29.8 7.8 %all-to-all-start = ((bf16[4,16,24,2048]{3,2,0,1:T(8,128)(2,1)}), bf16[4,16,24,2048]{3,2,0,1:T(8,128)(2,1)}, u32[]{:S(2)}, u32[]{:S(2)}) async-start(bf16[4,16,24,2048]{3,2,0,1:T(8,128)(2,1)} %copy.47), calls=%async_computation | async-start | bytes 12582912 | tf_op jit(solution)/shard_map/all_to_all | solution.py:41
  37.6 0.1 copy.49
  37.7 0.1 reshape.87
  37.8 0.0 copy-done.1
  37.8 1.2 fusion.70
  39.0 90.8 %all-to-all-done = bf16[4,16,24,2048]{3,2,0,1:T(8,128)(2,1)} async-done(((bf16[4,16,24,2048]{3,2,0,1:T(8,128)(2,1)}), bf16[4,16,24,2048]{3,2,0,1:T(8,128)(2,1)}, u32[]{:S(2)}, u32[]{:S(2)}) %all-to-all-start) | async-done | bytes 6291488 | tf_op jit(solution)/shard_map/all_to_all | solution.py:41
  129.9 4.8 %fusion.69 = (bf16[1,16,24,2048]{3,2,0,1:T(8,128)(2,1)S(1)}, bf16[1,16,24,2048]{3,2,0,1:T(8,128)(2,1)}, bf16[1,16,24,2048]{3,2,0,1:T(8,128)(2,1)S(1)}, bf16[1,16,24,2048]{3,2,0,1:T(8,128)(2,1)S(1)}) fusion(bf16[4,16,24,2048]{3,2,0,1:T(8,128)(2,1)} %all-to-all-done), kind=kLoop, calls=%fused_computation.80 | loop fusion | bytes 12582912 | tf_op jit(solution)/shard_map/slice | solution.py:47
  134.7 0.0 copy-done.8
  134.7 3.5 fusion.23
  138.2 3.6 multiply_reduce_fusion.2
  141.8 0.0 slice-done
  141.8 0.0 slice-done.1
  141.8 0.0 copy-done.7
  141.8 0.0 slice-done.2
  141.9 1.5 multiply_reduce_fusion.1
  143.4 0.0 copy-done.2
  143.4 0.0 copy-start.6
  143.4 3.5 fusion.24
  146.9 1.5 multiply_reduce_fusion.3
  148.4 3.5 fusion.22
  151.9 0.1 stack.61
  152.0 0.1 stack.62
  152.1 0.1 stack.60
  152.2 3.9 %multiply_reduce_fusion = f32[384]{0:T(512)S(1)} fusion(bf16[384,2048]{1,0:T(8,128)(2,1)} %bitcast.95, bf16[384,768]{1,0:T(8,128)(2,1)S(1)} %bitcast.98, bf16[4,2048,768]{2,1,0:T(8,128)(2,1)} %param.12), kind=kOutput, calls=%fused_computation.28 | convolution fusion | flops 1210318464 | bytes 5309952 | tf_op jit(solution)/shard_map/dot_general | solution.py:50
  156.1 0.1 stack.63
  156.2 0.7 pad_maximum_fusion.2
  156.9 5.4 %all-to-all-start.1 = ((f32[4,16,24]{2,0,1:T(4,128)}), f32[4,16,24]{2,0,1:T(4,128)S(1)}, u32[]{:S(2)}, u32[]{:S(2)}) async-start(f32[4,16,24]{2,0,1:T(4,128)} %pad_maximum_fusion.2), calls=%async_computation.2 | async-start | bytes 65536 | tf_op jit(solution)/shard_map/all_to_all | solution.py:67
  162.3 0.3 all-reduce.2.cloned.1.call-start
  162.6 4.9 %fusion.25 = bf16[1,2048,768]{2,1,0:T(8,128)(2,1)} fusion(bf16[384,2048]{1,0:T(8,128)(2,1)} %bitcast.96, bf16[384,768]{1,0:T(8,128)(2,1)S(1)} %bitcast.99), kind=kOutput, calls=%fused_computation.36 | convolution fusion | flops 1209532416 | bytes 5308416 | tf_op jit(solution)/shard_map/dot_general | solution.py:58
  167.5 1.3 all-to-all-done.1
  168.7 0.1 reshape.84
  168.8 0.0 copy-start.11
  168.8 0.0 copy-start.10
  168.8 6.2 %gather_fusion = f32[1024]{0:T(1024)S(1)} fusion(f32[1536]{0:T(1024)S(1)} %reshape.84, s32[1024]{0:T(1024)S(1)} %broadcast_clamp_fusion), kind=kCustom, calls=%fused_computation | custom fusion | bytes 12288 | tf_op jit(solution)/shard_map/gather | solution.py:69
  175.0 0.1 reshape.86
  175.1 0.1 reduce_sum.81
  175.3 0.0 copy-done.11
  175.4 1.0 fusion.71
  176.4 0.0 all-reduce.2.cloned.1.call-update
  176.4 0.0 reduce-scatter.2.cloned.1.call-start
  176.5 10.7 %pad_maximum_fusion = bf16[4,2048,768]{2,1,0:T(8,128)(2,1)} fusion(bf16[1,2048,768]{2,1,0:T(8,128)(2,1)} %fusion.25, bf16[1,2048,768]{2,1,0:T(8,128)(2,1)} %fusion.24, bf16[1,2048,768]{2,1,0:T(8,128)(2,1)} %fusion.23, bf16[1,2048,768]{2,1,0:T(8,128)(2,1)} %fusion.22), kind=kLoop, calls=%fused_computation.2 | loop fusion | flops 18874368 | bytes 25165824 | tf_op jit(solution)/shard_map/stack | solution.py:63
  187.2 0.0 reduce-scatter.2.cloned.1.call-update
  187.2 3.9 %fusion.51 = bf16[384,768]{1,0:T(8,128)(2,1)S(1)} fusion(bf16[384,2048]{1,0:T(8,128)(2,1)} %bitcast.97, bf16[4,2048,768]{2,1,0:T(8,128)(2,1)} %param.12), kind=kOutput, calls=%fused_computation.50 | convolution fusion | flops 1208254464 | bytes 5308416 | tf_op jit(solution)/shard_map/dot_general | solution.py:55
  191.1 3.4 fusion.42
  194.6 3.3 fusion.48
  197.9 4.1 %fusion.45 = bf16[384,768]{1,0:T(8,128)(2,1)S(1)} fusion(bf16[384,2048]{1,0:T(8,128)(2,1)S(1)} %bitcast.88, bf16[4,2048,768]{2,1,0:T(8,128)(2,1)} %param.12), kind=kOutput, calls=%fused_computation.48 | convolution fusion | flops 1208254464 | bytes 5308416 | tf_op jit(solution)/shard_map/dot_general | solution.py:55
  202.0 0.0 copy-start.9
  202.0 1.7 pad_maximum_fusion.1
  203.7 0.0 copy-done.9
  203.7 1.1 convolution_convert_fusion.4
  204.9 152.0 %all-reduce.2.cloned.1.call-done = f32[64,2048]{1,0:T(8,128)} async-done(((f32[64,2048]{1,0:T(8,128)}), f32[64,2048]{1,0:T(8,128)}) %all-reduce.2.cloned.1.call-update) | async-done | bytes 524304 | tf_op jit(solution)/shard_map/psum | solution.py:80
  356.9 1.9 copy.52
  (24 shorter events, 0.1 us)
Async XLA Ops:
  8.0 167.4 %copy-start = (bf16[128,2048]{1,0:T(8,128)(2,1)S(1)}, bf16[128,2048]{1,0:T(8,128)(2,1)}, u32[]{:S(2)}) copy-start(bf16[128,2048]{1,0:T(8,128)(2,1)} %param.7) | copy-start | bytes 1572868
  29.8 8.0 %copy-start.1 = (bf16[1,4,16,24,768]{4,3,2,1,0:T(8,128)(2,1)S(1)}, bf16[1,4,16,24,768]{4,3,2,1,0:T(8,128)(2,1)}, u32[]{:S(2)}) copy-start(bf16[1,4,16,24,768]{4,3,2,1,0:T(8,128)(2,1)} %param.11) | copy-start | bytes 7077892
  29.8 100.1 %all-to-all-start = ((bf16[4,16,24,2048]{3,2,0,1:T(8,128)(2,1)}), bf16[4,16,24,2048]{3,2,0,1:T(8,128)(2,1)}, u32[]{:S(2)}, u32[]{:S(2)}) async-start(bf16[4,16,24,2048]{3,2,0,1:T(8,128)(2,1)} %copy.47), calls=%async_computation | async-start | bytes 12582912 | tf_op jit(solution)/shard_map/all_to_all | solution.py:41
  39.0 95.7 %copy-start.8 = (bf16[1,1,16,24,768]{4,3,2,1,0:T(8,128)(2,1)S(1)}, bf16[1,1,16,24,768]{4,3,2,1,0:T(8,128)(2,1)}, u32[]{:S(2)}) copy-start(bf16[1,1,16,24,768]{4,3,2,1,0:T(8,128)(2,1)} %get-tuple-element.11) | copy-start | bytes 1769476
  129.9 11.9 %slice-start = ((s8[12582912]{0:T(1024)(128)(4,1)}), s8[4194304]{0:T(1024)(128)(4,1)S(1)}, s32[]{:S(2)}) async-start(s8[12582912]{0:T(1024)(128)(4,1)} %bitcast.111), calls=%async_computation.5 | async-start | bytes 8388608
  129.9 11.9 %slice-start.1 = ((s8[12582912]{0:T(1024)(128)(4,1)}), s8[4194304]{0:T(1024)(128)(4,1)S(1)}, s32[]{:S(2)}) async-start(s8[12582912]{0:T(1024)(128)(4,1)} %bitcast.111), calls=%async_computation.6 | async-start | bytes 8388608
  134.7 8.7 %copy-start.2 = (bf16[1,16,24,2048]{3,2,0,1:T(8,128)(2,1)}, bf16[1,16,24,2048]{3,2,0,1:T(8,128)(2,1)S(1)}, u32[]{:S(2)}) copy-start(bf16[1,16,24,2048]{3,2,0,1:T(8,128)(2,1)S(1)} %get-tuple-element.8) | copy-start | bytes 4718596
  134.7 13.7 %copy-start.4 = (bf16[1,16,24,2048]{3,2,0,1:T(8,128)(2,1)}, bf16[1,16,24,2048]{3,2,0,1:T(8,128)(2,1)S(1)}, u32[]{:S(2)}) copy-start(bf16[1,16,24,2048]{3,2,0,1:T(8,128)(2,1)S(1)} %get-tuple-element.6) | copy-start | bytes 4718596
  138.2 3.6 copy-start.7
  138.2 3.6 slice-start.2
  143.4 3.5 copy-start.6
  156.9 11.8 %all-to-all-start.1 = ((f32[4,16,24]{2,0,1:T(4,128)}), f32[4,16,24]{2,0,1:T(4,128)S(1)}, u32[]{:S(2)}, u32[]{:S(2)}) async-start(f32[4,16,24]{2,0,1:T(4,128)} %pad_maximum_fusion.2), calls=%async_computation.2 | async-start | bytes 65536 | tf_op jit(solution)/shard_map/all_to_all | solution.py:67
  162.3 194.6 %all-reduce.2.cloned.1.call-start = ((), (), s32[]{:S(2)}) async-start(), calls=%async_computation.4 | async-start | bytes 1048576 | tf_op jit(solution)/shard_map/psum | solution.py:80
  168.8 6.5 %copy-start.11 = (f32[128,8]{0,1:T(8,128)S(1)}, f32[128,8]{0,1:T(8,128)}, u32[]{:S(2)}) copy-start(f32[128,8]{0,1:T(8,128)} %param.9) | copy-start | bytes 12292
  168.8 6.5 %copy-start.10 = (s32[128,8]{0,1:T(8,128)S(1)}, s32[128,8]{0,1:T(8,128)}, u32[]{:S(2)}) copy-start(s32[128,8]{0,1:T(8,128)} %param.10) | copy-start | bytes 12292
  176.4 180.5 %reduce-scatter.2.cloned.1.call-start = ((), (), s32[]{:S(2)}) async-start(), calls=%async_computation.3 | async-start | bytes 14155776 | tf_op jit(solution)/shard_map/reduce_scatter | solution.py:62
  187.2 3.9 %copy-start.5 = (bf16[1,16,24,2048]{3,2,0,1:T(8,128)(2,1)S(1)}, bf16[1,16,24,2048]{3,2,0,1:T(8,128)(2,1)}, u32[]{:S(2)}) copy-start(bf16[1,16,24,2048]{3,2,0,1:T(8,128)(2,1)} %copy-done.4) | copy-start | bytes 4718596
  191.1 3.5 copy-start.3
  202.0 1.7 copy-start.9
Sparse Core Ops, SparseCore 0:
  176.5 180.2 all-reduce.1
Sparse Core Ops, SparseCore 1:
  187.3 75.3 reduce-scatter.1
where the time goes:
time: 367 us; the launch traced here: 366 us
  waiting for transfers between devices  244 us (66%)
  matrix products  43 us (12%)
  other arithmetic  27.2 us (7%)
  local copies, waits for them, and re-layouts  22.6 us (6%)
  between operations  15.8 us (4%)
  starting transfers between devices  13.5 us (4%)
    psum x1, waiting for transfers between devices, local(): router_grad = lax.psum(router_part, ('dp', 'expert'))  152 us
    all_to_all x1, waiting for transfers between devices, local(): lax.all_to_all(packed, 'expert', split_axis=1, concat_axis=1, tiled=True)  90.8 us
    dot_general x4, matrix products, local(): lax.dot_general(slot_rows, slot_acts, (((0,), (0,)), ((), ())), preferred...  15.5 us
    dot_general x4, matrix products, local(): jnp.dot(slot_rows, weight, preferred_element_type=jnp.float32)  14.8 us
    another operation x1, other arithmetic, local(): jnp.stack(weight_terms).astype(jnp.bfloat16)  10.7 us
    scatter x1, other arithmetic, pack_rows(): filled = zero_rows.at[flat_index.reshape(-1)].set(scaled.reshape(-1, width))  10.6 us
    dot_general x4, matrix products, local(): lax.dot_general(slot_acts, weight, (((1,), (1,)), ((), ())), preferred_el...  10.5 us
    all_to_all x1, starting transfers between devices, local(): lax.all_to_all(packed, 'expert', split_axis=1, concat_axis=1, tiled=True)  7.77 us
  transfers between devices with their start and end apart: 4, of which 3 were waited for; matrix products, arithmetic and copies ran while one was open for 9% of the time, Pallas kernels for 0%

commit v1 on v0

--- a/solution.py
+++ b/solution.py
@@ -2,6 +2,7 @@
 import jax.numpy as jnp
 from jax import lax
 from jax.sharding import PartitionSpec as P
+from jax.lax import psum
 
 
 def make_marks(block_routes, total_experts):
@@ -77,7 +78,7 @@
     router_part = lax.dot_general(
         dense_grad, inputs, (((0,), (0,)), ((), ())), preferred_element_type=jnp.float32
     )
-    router_grad = lax.psum(router_part, ("dp", "expert"))
+    router_grad = psum(psum(router_part, axis_name="expert"), axis_name="dp")
     return (hidden_grad, down_grad, input_grad, router_grad)
 
 

time: 367 us -> 407 us (1.11)
  waiting for transfers between devices: 244 us -> 280 us
  matrix products: 43 us -> 48.6 us
    reduce_scatter x1, waiting for transfers between devices: 0.01 us -> 76 us  [local(): lax.psum_scatter(jnp.stack(weight_terms).astype(jnp.bfloat16), 'dp', scat...]
    psum x1 -> x2, waiting for transfers between devices: 152 us -> 112 us  [local(): router_grad = psum(psum(router_part, axis_name='expert'), axis_name='dp')]
    dot_general x4, matrix products: 10.5 us -> 15.3 us  [local(): lax.dot_general(slot_acts, weight, (((1,), (1,)), ((), ())), preferred_el...]
  transfers between devices with their start and end apart: 4 -> 5, of which waited for: 3 -> 5; matrix products, arithmetic and copies ran while one was open for 9% -> 10% of each run, Pallas kernels for 0% -> 0%
where the time goes in v1:
time: 407 us
  waiting for transfers between devices  280 us (69%)
  matrix products  48.6 us (12%)
  other arithmetic  27.2 us (7%)
  local copies, waits for them, and re-layouts  23.1 us (6%)
  between operations  14 us (3%)
  starting transfers between devices  13.5 us (3%)
    psum x2, waiting for transfers between devices, local(): router_grad = psum(psum(router_part, axis_name='expert'), axis_name='dp')  112 us
    all_to_all x1, waiting for transfers between devices, local(): lax.all_to_all(packed, 'expert', split_axis=1, concat_axis=1, tiled=True)  90.8 us
    reduce_scatter x1, waiting for transfers between devices, local(): lax.psum_scatter(jnp.stack(weight_terms).astype(jnp.bfloat16), 'dp', scat...  76 us
    dot_general x4, matrix products, local(): lax.dot_general(slot_rows, slot_acts, (((0,), (0,)), ((), ())), preferred...  17.1 us
    dot_general x4, matrix products, local(): lax.dot_general(slot_acts, weight, (((1,), (1,)), ((), ())), preferred_el...  15.3 us
    dot_general x4, matrix products, local(): jnp.dot(slot_rows, weight, preferred_element_type=jnp.float32)  13.9 us
    another operation x1, other arithmetic, local(): jnp.stack(weight_terms).astype(jnp.bfloat16)  10.7 us
    scatter x1, other arithmetic, pack_rows(): filled = zero_rows.at[flat_index.reshape(-1)].set(scaled.reshape(-1, width))  10.6 us
  transfers between devices with their start and end apart: 5, of which 5 were waited for; matrix products, arithmetic and copies ran while one was open for 10% of the time, Pallas kernels for 0%

profile of v1, /device:TPU:1, one launch (start us, length us, event | category | flops | bytes accessed | tf_op | source)
XLA Modules:
  0.0 406.7 jit_solution(740968120174877481)
XLA Ops:
  7.2 0.0 copy-start
  7.2 0.8 fusion.55
  8.0 0.1 fusion.56
  8.1 0.7 select_reduce_fusion.1
  8.8 0.7 compare_select_fusion.1
  9.6 0.1 copy.45
  9.7 0.1 reshape.82
  9.8 0.8 copy.46
  10.6 0.1 mul.48
  10.6 1.1 convert_element_type.50
  11.8 10.6 %scatter_custom_fusion = bf16[1536,2048]{1,0:T(8,128)(2,1)} fusion(s32[1024]{0:T(1024)S(1)} %bitcast.110, f32[128,2048]{1,0:T(8,128)S(1)} %convert_element_type.50, f32[1024]{0:T(1024)S(1)} %mul.48, bf16[]{:T(256)} %constant.31.clone.1), kind=kCustom, calls=%fused_computation.5 | custom fusion | flops 4194304 | bytes 7344130 | tf_op jit(solution)/shard_map/scatter | solution.py:25
  22.4 6.6 %copy.47 = bf16[4,16,24,2048]{3,2,0,1:T(8,128)(2,1)} copy(bf16[4,16,24,2048]{3,2,1,0:T(8,128)(2,1)} %bitcast.85) | data formatting | bytes 12582912 | tf_op jit(solution)/shard_map/reshape | solution.py:26
  29.0 7.8 %all-to-all-start = ((bf16[4,16,24,2048]{3,2,0,1:T(8,128)(2,1)}), bf16[4,16,24,2048]{3,2,0,1:T(8,128)(2,1)}, u32[]{:S(2)}, u32[]{:S(2)}) async-start(bf16[4,16,24,2048]{3,2,0,1:T(8,128)(2,1)} %copy.47), calls=%async_computation | async-start | bytes 12582912 | tf_op jit(solution)/shard_map/all_to_all | solution.py:42
  36.7 0.1 copy.49
  36.8 0.1 reshape.87
  37.0 1.2 fusion.70
  38.2 90.8 %all-to-all-done = bf16[4,16,24,2048]{3,2,0,1:T(8,128)(2,1)} async-done(((bf16[4,16,24,2048]{3,2,0,1:T(8,128)(2,1)}), bf16[4,16,24,2048]{3,2,0,1:T(8,128)(2,1)}, u32[]{:S(2)}, u32[]{:S(2)}) %all-to-all-start) | async-done | bytes 6291488 | tf_op jit(solution)/shard_map/all_to_all | solution.py:42
  129.0 5.3 %fusion.69 = (bf16[1,16,24,2048]{3,2,0,1:T(8,128)(2,1)}, bf16[1,16,24,2048]{3,2,0,1:T(8,128)(2,1)}, bf16[1,16,24,2048]{3,2,0,1:T(8,128)(2,1)}, bf16[1,16,24,2048]{3,2,0,1:T(8,128)(2,1)S(1)}) fusion(bf16[4,16,24,2048]{3,2,0,1:T(8,128)(2,1)} %all-to-all-done), kind=kLoop, calls=%fused_computation.80 | loop fusion | bytes 12582912 | tf_op jit(solution)/shard_map/slice | solution.py:48
  134.3 0.0 copy-done.6
  134.3 3.5 fusion.23
  137.8 3.4 multiply_reduce_fusion.2
  141.3 0.1 stack.61
  141.4 0.0 copy-start.5
  141.4 4.1 %multiply_reduce_fusion.1 = f32[384]{0:T(512)S(1)} fusion(bf16[384,2048]{1,0:T(8,128)(2,1)} %bitcast.89, bf16[384,768]{1,0:T(8,128)(2,1)} %bitcast.102, bf16[4,2048,768]{2,1,0:T(8,128)(2,1)} %param.12), kind=kOutput, calls=%fused_computation.29 | convolution fusion | flops 1210318464 | bytes 5309952 | tf_op jit(solution)/shard_map/dot_general | solution.py:51
  145.5 0.1 stack.62
  145.6 3.9 multiply_reduce_fusion.3
  149.5 0.1 stack.60
  149.6 3.9 multiply_reduce_fusion
  153.5 0.1 stack.63
  153.6 0.7 pad_maximum_fusion.2
  154.2 5.4 %all-to-all-start.1 = ((f32[4,16,24]{2,0,1:T(4,128)}), f32[4,16,24]{2,0,1:T(4,128)S(1)}, u32[]{:S(2)}, u32[]{:S(2)}) async-start(f32[4,16,24]{2,0,1:T(4,128)} %pad_maximum_fusion.2), calls=%async_computation.2 | async-start | bytes 65536 | tf_op jit(solution)/shard_map/all_to_all | solution.py:68
  159.6 0.0 all-reduce.3.cloned.1.call-start
  159.7 5.0 %fusion.24 = bf16[1,2048,768]{2,1,0:T(8,128)(2,1)} fusion(bf16[384,2048]{1,0:T(8,128)(2,1)} %bitcast.90, bf16[384,768]{1,0:T(8,128)(2,1)} %bitcast.103), kind=kOutput, calls=%fused_computation.35 | convolution fusion | flops 1209532416 | bytes 5308416 | tf_op jit(solution)/shard_map/dot_general | solution.py:59
  164.7 1.4 all-to-all-done.1
  166.1 0.1 reshape.84
  166.2 0.0 copy-start.9
  166.2 0.0 copy-start.8
  166.2 6.2 %gather_fusion = f32[1024]{0:T(1024)S(1)} fusion(f32[1536]{0:T(1024)S(1)} %reshape.84, s32[1024]{0:T(1024)S(1)} %broadcast_clamp_fusion), kind=kCustom, calls=%fused_computation | custom fusion | bytes 12288 | tf_op jit(solution)/shard_map/gather | solution.py:70
  172.3 0.1 reshape.86
  172.5 0.1 reduce_sum.81
  172.7 0.0 copy-done
  172.7 1.0 fusion.71
  173.7 0.0 all-reduce.3.cloned.1.call-update
  173.7 0.3 all-reduce.5.cloned.1.call-start
  174.0 0.0 copy-start.4
  174.0 5.0 %fusion.22 = bf16[1,2048,768]{2,1,0:T(8,128)(2,1)} fusion(bf16[384,2048]{1,0:T(8,128)(2,1)} %bitcast.93, bf16[384,768]{1,0:T(8,128)(2,1)S(1)} %bitcast.101), kind=kOutput, calls=%fused_computation.33 | convolution fusion | flops 1209532416 | bytes 5308416 | tf_op jit(solution)/shard_map/dot_general | solution.py:59
  179.0 3.5 fusion.25
  182.6 77.6 %all-reduce.3.cloned.1.call-done = f32[64,2048]{1,0:T(8,128)} async-done(((f32[64,2048]{1,0:T(8,128)}), f32[64,2048]{1,0:T(8,128)}) %all-reduce.3.cloned.1.call-update) | async-done | bytes 524304 | tf_op jit(solution)/shard_map/psum | solution.py:81
  260.2 0.0 all-reduce.5.cloned.1.call-update
  260.2 0.0 reduce-scatter.2.cloned.1.call-start
  260.2 10.7 %pad_maximum_fusion = bf16[4,2048,768]{2,1,0:T(8,128)(2,1)} fusion(bf16[1,2048,768]{2,1,0:T(8,128)(2,1)} %fusion.25, bf16[1,2048,768]{2,1,0:T(8,128)(2,1)} %fusion.24, bf16[1,2048,768]{2,1,0:T(8,128)(2,1)} %fusion.23, bf16[1,2048,768]{2,1,0:T(8,128)(2,1)} %fusion.22), kind=kLoop, calls=%fused_computation.2 | loop fusion | flops 18874368 | bytes 25165824 | tf_op jit(solution)/shard_map/stack | solution.py:64
  270.9 0.0 reduce-scatter.2.cloned.1.call-update
  271.0 0.0 copy-start.3
  271.0 3.9 fusion.51
  274.9 3.4 fusion.42
  278.3 0.0 copy-done.2
  278.3 3.3 fusion.48
  281.7 3.3 fusion.45
  285.0 0.0 copy-start.7
  285.0 1.7 pad_maximum_fusion.1
  286.7 1.1 convolution_convert_fusion.4
  287.8 34.5 %all-reduce.5.cloned.1.call-done = f32[64,2048]{1,0:T(8,128)} async-done(((f32[64,2048]{1,0:T(8,128)}), f32[64,2048]{1,0:T(8,128)}) %all-reduce.5.cloned.1.call-update) | async-done | bytes 524304 | tf_op jit(solution)/shard_map/psum | solution.py:81
  322.3 76.0 %reduce-scatter.2.cloned.1.call-done = bf16[4,256,768]{2,1,0:T(8,128)(2,1)} async-done(((bf16[4,2048,768]{2,1,0:T(8,128)(2,1)}), bf16[4,256,768]{2,1,0:T(8,128)(2,1)}) %reduce-scatter.2.cloned.1.call-update) | async-done | bytes 1572880 | tf_op jit(solution)/shard_map/reduce_scatter | solution.py:63
  398.3 1.9 copy.53
  (16 shorter events, 0.1 us)
Async XLA Ops:
  7.2 165.5 %copy-start = (bf16[128,2048]{1,0:T(8,128)(2,1)S(1)}, bf16[128,2048]{1,0:T(8,128)(2,1)}, u32[]{:S(2)}) copy-start(bf16[128,2048]{1,0:T(8,128)(2,1)} %param.7) | copy-start | bytes 1572868
  29.0 8.0 %copy-start.1 = (bf16[1,4,16,24,768]{4,3,2,1,0:T(8,128)(2,1)S(1)}, bf16[1,4,16,24,768]{4,3,2,1,0:T(8,128)(2,1)}, u32[]{:S(2)}) copy-start(bf16[1,4,16,24,768]{4,3,2,1,0:T(8,128)(2,1)} %param.11) | copy-start | bytes 7077892
  29.0 100.1 %all-to-all-start = ((bf16[4,16,24,2048]{3,2,0,1:T(8,128)(2,1)}), bf16[4,16,24,2048]{3,2,0,1:T(8,128)(2,1)}, u32[]{:S(2)}, u32[]{:S(2)}) async-start(bf16[4,16,24,2048]{3,2,0,1:T(8,128)(2,1)} %copy.47), calls=%async_computation | async-start | bytes 12582912 | tf_op jit(solution)/shard_map/all_to_all | solution.py:42
  38.2 96.1 %copy-start.6 = (bf16[1,1,16,24,768]{4,3,2,1,0:T(8,128)(2,1)S(1)}, bf16[1,1,16,24,768]{4,3,2,1,0:T(8,128)(2,1)}, u32[]{:S(2)}) copy-start(bf16[1,1,16,24,768]{4,3,2,1,0:T(8,128)(2,1)} %get-tuple-element.11) | copy-start | bytes 1769476
  141.4 4.2 %copy-start.5 = (bf16[1,1,16,24,768]{4,3,2,1,0:T(8,128)(2,1)S(1)}, bf16[1,1,16,24,768]{4,3,2,1,0:T(8,128)(2,1)}, u32[]{:S(2)}) copy-start(bf16[1,1,16,24,768]{4,3,2,1,0:T(8,128)(2,1)} %get-tuple-element.10) | copy-start | bytes 1769476
  154.2 11.8 %all-to-all-start.1 = ((f32[4,16,24]{2,0,1:T(4,128)}), f32[4,16,24]{2,0,1:T(4,128)S(1)}, u32[]{:S(2)}, u32[]{:S(2)}) async-start(f32[4,16,24]{2,0,1:T(4,128)} %pad_maximum_fusion.2), calls=%async_computation.2 | async-start | bytes 65536 | tf_op jit(solution)/shard_map/all_to_all | solution.py:68
  159.6 100.6 %all-reduce.3.cloned.1.call-start = ((), (), s32[]{:S(2)}) async-start(), calls=%async_computation.4 | async-start | bytes 1048576 | tf_op jit(solution)/shard_map/psum | solution.py:81
  166.2 6.5 %copy-start.9 = (f32[128,8]{0,1:T(8,128)S(1)}, f32[128,8]{0,1:T(8,128)}, u32[]{:S(2)}) copy-start(f32[128,8]{0,1:T(8,128)} %param.9) | copy-start | bytes 12292
  166.2 6.5 %copy-start.8 = (s32[128,8]{0,1:T(8,128)S(1)}, s32[128,8]{0,1:T(8,128)}, u32[]{:S(2)}) copy-start(s32[128,8]{0,1:T(8,128)} %param.10) | copy-start | bytes 12292
  173.7 148.5 %all-reduce.5.cloned.1.call-start = ((), (), s32[]{:S(2)}) async-start(), calls=%async_computation.5 | async-start | bytes 1048576 | tf_op jit(solution)/shard_map/psum | solution.py:81
  174.0 5.0 %copy-start.4 = (bf16[1,16,24,2048]{3,2,0,1:T(8,128)(2,1)S(1)}, bf16[1,16,24,2048]{3,2,0,1:T(8,128)(2,1)}, u32[]{:S(2)}) copy-start(bf16[1,16,24,2048]{3,2,0,1:T(8,128)(2,1)} %get-tuple-element.7) | copy-start | bytes 4718596
  260.2 138.1 %reduce-scatter.2.cloned.1.call-start = ((), (), s32[]{:S(2)}) async-start(), calls=%async_computation.3 | async-start | bytes 14155776 | tf_op jit(solution)/shard_map/reduce_scatter | solution.py:63
  271.0 3.9 copy-start.3
  274.9 3.4 copy-start.2
  285.0 1.7 copy-start.7
Sparse Core Ops, SparseCore 0:
  173.8 86.2 all-reduce.2
  262.6 59.6 all-reduce.4
  325.3 72.9 reduce-scatter.1
